TPU v7x, 32 devices: a whole 2x2x4 slice. The times are simulated.
32 devices in a mesh: shot: 4 (over y, core), depth: 8 (over z, x).
Axes of the slice: x: 2, y: 2, z: 4, core: 2. Of those that a mesh axis runs over, the one named last changes fastest.
Arguments:
- grad_part: float32 [4, 256, 8192], P('shot', 'depth'), may hold values from -6 to 6
- illum_part: float32 [4, 256, 8192], P('shot', 'depth'), may hold values from 0.1 to 1
- source_count: int32 [4], P('shot'), may hold values from 1 to 8
- rate: float32 [8192], P('shot'), may hold values from 0.00078125 to 0.03
- coef_table: float32 [64], replicated, may hold values from 0.2 to 1
- coef_index: int32 [256], P('depth'), may hold values from 0 to 63
Outputs:
- image: float32 [256, 8192], P('depth', 'shot')
All inputs are finite; a program needn't handle non-finite values.
Results may differ from a plain program's by a relative error of at most 0.0003.
Values sent between devices are 32-bit elements; how exact they have to be, the bound alone decides.
A program may use at most 64 MiB of HBM per device.

v0:
```python
import functools

import jax
import jax.numpy as jnp
from jax import lax
from jax.experimental import pallas as pl
from jax.experimental.pallas import tpu as pltpu
from jax.sharding import PartitionSpec as P

MESH = pl.DeviceIdType.MESH
LANES = 128
SUB = 8


def body(
    dims,
    grad, illum, weight, rate, table, index, out,
    own, part, sums, landed, early, late, inject, weigh, back, reach, held, states, theirs,
    own_sem, part_send, part_recv, sums_send, sums_recv,
    early_send, early_recv, late_send, late_recv, w_send, w_recv, word,
):
    ys, ks, rows, width, counts = dims
    chunks = len(counts)
    starts = [sum(counts[:ch]) for ch in range(chunks)]
    tiles = rows // SUB
    me = lax.axis_index("shot")
    d = lax.axis_index("depth")
    y, c = me // 2, me % 2
    mate = y * 2 + 1 - c

    def peer(i):
        return lax.rem(d + i, ks)

    def other(i):
        return lax.rem(y + i, ys)

    def greet(semaphore):
        flip = d + 1 - 2 * lax.rem(d, 2)
        pl.semaphore_signal(semaphore, inc=1, device_id=(me, flip), device_id_type=MESH)
        for step in (2, -2):
            near = d + step

            @pl.when((near >= 0) & (near < ks))
            def _():
                pl.semaphore_signal(semaphore, inc=1, device_id=(me, near), device_id_type=MESH)

    def greeted(semaphore, more):
        inner = (d >= 2).astype(jnp.int32) + (d < ks - 2).astype(jnp.int32)
        pl.semaphore_wait(semaphore, inner + 1 + more)

    barrier = pltpu.get_barrier_semaphore()
    pl.semaphore_signal(barrier, inc=1, device_id=(mate, d), device_id_type=MESH)
    for i in range(1, ys):
        pl.semaphore_signal(barrier, inc=1, device_id=(other(i) * 2 + c, d), device_id_type=MESH)
    greet(barrier)

    def slab(src, target, core, ch):
        at = pl.multiple_of((target * 2 + core) * width + starts[ch] * LANES, LANES)
        return src.at[0, :, pl.ds(at, counts[ch] * LANES)]

    def span(ch):
        return pl.ds(0, counts[ch] * LANES)

    order = [(i, ch) for i in [*range(1, ys), 0] for ch in range(chunks)]

    def own_copy(i, ch, a):
        return pltpu.make_async_copy(
            slab((grad, illum)[a], other(i), c, ch), own.at[i, ch, a, :, span(ch)], own_sem.at[i, ch, a]
        )

    def part_copy(i, ch, a):
        return pltpu.make_async_remote_copy(
            src_ref=slab((grad, illum)[a], other(i), 1 - c, ch),
            dst_ref=part.at[i, ch, a, :, span(ch)],
            send_sem=part_send.at[i, ch, a],
            recv_sem=part_recv.at[i, ch, a],
            device_id=(mate, d),
            device_id_type=MESH,
        )

    def sums_copy(i, ch):
        return pltpu.make_async_remote_copy(
            src_ref=sums.at[i - 1, ch, :, :, span(ch)],
            dst_ref=landed.at[i - 1, ch, :, :, span(ch)],
            send_sem=sums_send.at[i - 1, ch],
            recv_sem=sums_recv.at[i - 1, ch],
            device_id=(other(i) * 2 + c, d),
            device_id_type=MESH,
        )

    def early_copy(i):
        return pltpu.make_async_remote_copy(
            src_ref=early.at[0],
            dst_ref=early.at[ks - i],
            send_sem=early_send.at[i - 1],
            recv_sem=early_recv.at[ks - i - 1],
            device_id=(me, peer(i)),
            device_id_type=MESH,
        )

    def late_copy(i, ch):
        return pltpu.make_async_remote_copy(
            src_ref=late.at[0, ch],
            dst_ref=late.at[ks - i, ch],
            send_sem=late_send.at[i - 1, ch],
            recv_sem=late_recv.at[ks - i - 1, ch],
            device_id=(me, peer(i)),
            device_id_type=MESH,
        )

    w_copy = pltpu.make_async_remote_copy(
        src_ref=weight,
        dst_ref=theirs,
        send_sem=w_send,
        recv_sem=w_recv,
        device_id=(mate, d),
        device_id_type=MESH,
    )

    first_part, second_part = order[: (ys - 1) * chunks], order[(ys - 1) * chunks :]
    for i, ch in first_part:
        for a in range(2):
            own_copy(i, ch, a).start()

    greeted(barrier, ys)
    w_copy.start()
    for i, ch in first_part:
        for a in range(2):
            part_copy(i, ch, a).start()

    rounds = ks // 2 - 1
    greet(word.at[0])

    def pass_on(r):
        greeted(word.at[r], 0)
        if r + 1 < rounds:
            greet(word.at[r + 1])

    sub = lax.broadcasted_iota(jnp.int32, (SUB, LANES), 0)

    def prefix(v):
        for s in (1, 2, 4):
            v = v + jnp.where(sub >= s, pltpu.roll(v, s, 0), 0.0)
        return v

    def suffix(v):
        for s in (1, 2, 4):
            v = v + jnp.where(sub < SUB - s, pltpu.roll(v, SUB - s, 0), 0.0)
        return v

    def first(v):
        return jnp.broadcast_to(v[0:1], (SUB, LANES))

    def last(v):
        return jnp.broadcast_to(v[SUB - 1 : SUB], (SUB, LANES))

    entries = table.shape[1]

    def upright(row):
        n = row.shape[1]
        diagonal = lax.broadcasted_iota(jnp.int32, (n, n), 0) == lax.broadcasted_iota(
            jnp.int32, (n, n), 1
        )
        return jnp.sum(
            jnp.where(diagonal, jnp.broadcast_to(row, (n, n)), 0.0), axis=1, keepdims=True
        )

    level = lax.broadcasted_iota(jnp.int32, (entries, rows), 0)
    hit = jnp.broadcast_to(index[...], (entries, rows)) == level
    spread = jnp.broadcast_to(upright(table[...]), (entries, rows))
    picked = upright(jnp.sum(jnp.where(hit, spread, 0.0), axis=0, keepdims=True))

    coef, through, before = [], [], []
    total = jnp.zeros((SUB, LANES), jnp.float32)
    for t in range(tiles):
        v = jnp.broadcast_to(picked[t * SUB : (t + 1) * SUB], (SUB, LANES))
        run = prefix(v) + total
        coef.append(v)
        through.append(run)
        before.append(run - v)
        total = last(run)

    def terms():
        for j in range(width // LANES):
            at = pl.ds(j * LANES, LANES)
            r = jnp.broadcast_to(rate[0:1, at], (SUB, LANES))
            tail = jnp.zeros((SUB, LANES), jnp.float32)
            for t in reversed(range(tiles)):
                zs = pl.ds(t * SUB, SUB)
                rest = 1.0 - jnp.exp(-(coef[t] * r))
                inject[zs, at] = rest * jnp.exp(through[t] * r)
                h = rest * jnp.exp(-((through[t] + before[t]) * r))
                weigh[zs, at] = h
                lift = jnp.exp(before[t] * r)
                back[zs, at] = lift
                run = suffix(h) + tail
                reach[zs, at] = lift * run
                tail = first(run)
            early[0, 0, pl.ds(j, 1), :] = jnp.exp(-(total * r))[0:1]
            early[0, 1, pl.ds(j, 1), :] = tail[0:1]

    def reduced(i, ch, a, zs, at):
        if a == 0:
            w, v = weight[...], theirs[...]
            return own[i, ch, 0, zs, at] * w + part[i, ch, 0, zs, at] * v
        return own[i, ch, 1, zs, at] + part[i, ch, 1, zs, at]

    def arrived(i, ch):
        for a in range(2):
            own_copy(i, ch, a).wait()
            part_copy(i, ch, a).wait_recv()

    w_copy.wait_recv()
    for n, (i, ch) in enumerate(first_part):
        arrived(i, ch)
        for j in range(counts[ch]):
            at = pl.ds(j * LANES, LANES)
            for t in range(tiles):
                zs = pl.ds(t * SUB, SUB)
                for a in range(2):
                    sums[i - 1, ch, a, zs, at] = reduced(i, ch, a, zs, at)
        sums_copy(i, ch).start()
        if n == 0:
            pass_on(0)

    for i, ch in second_part:
        for a in range(2):
            own_copy(i, ch, a).start()
            part_copy(i, ch, a).start()
    if rounds > 1:
        pass_on(1)
    terms()
    for r in range(2, rounds):
        pass_on(r)
    for i in range(1, ks):
        early_copy(i).start()

    for ch in range(chunks):
        arrived(0, ch)
        for i in range(1, ys):
            sums_copy(i, ch).wait_recv()
        for j in range(counts[ch]):
            at = pl.ds(j * LANES, LANES)
            full = pl.ds((starts[ch] + j) * LANES, LANES)
            carry = jnp.zeros((SUB, LANES), jnp.float32)
            parts = []
            for t in range(tiles):
                zs = pl.ds(t * SUB, SUB)
                num, den = reduced(0, ch, 0, zs, at), reduced(0, ch, 1, zs, at)
                for i in range(1, ys):
                    num = num + landed[i - 1, ch, 0, zs, at]
                    den = den + landed[i - 1, ch, 1, zs, at]
                run = prefix(inject[zs, full] * (num / den)) + carry
                parts.append(run)
                carry = last(run)
            row = pl.ds(starts[ch] + j, 1)
            late[0, ch, 0, pl.ds(j, 1), :] = carry[0:1] * early[0, 0, row, :]
            tail = jnp.zeros((SUB, LANES), jnp.float32)
            for t in reversed(range(tiles)):
                zs = pl.ds(t * SUB, SUB)
                run = suffix(weigh[zs, full] * parts[t]) + tail
                held[zs, full] = run
                tail = first(run)
            late[0, ch, 1, pl.ds(j, 1), :] = tail[0:1]
        for i in range(1, ks):
            late_copy(i, ch).start()

    for i in range(1, ks):
        early_copy(i).wait_recv()

    for ch in range(chunks):
        for i in range(1, ks):
            late_copy(i, ch).wait_recv()
        cols = counts[ch]
        rs = pl.ds(starts[ch], cols)
        state = jnp.zeros((cols, LANES), jnp.float32)
        mine = state
        ups = []
        for k in range(ks):
            slot = lax.rem(k - d + ks, ks)
            mine = jnp.where(k == d, state, mine)
            ups.append(late[slot, ch, 1, :cols] + early[slot, 1, rs] * state)
            if k < ks - 1:
                state = late[slot, ch, 0, :cols] + early[slot, 0, rs] * state
        up = jnp.zeros((cols, LANES), jnp.float32)
        for k in reversed(range(1, ks)):
            slot = lax.rem(k - d + ks, ks)
            up = jnp.where(k > d, ups[k] + early[slot, 0, rs] * up, up)
        states[0, rs] = mine
        states[1, rs] = up * early[0, 0, rs]
        for j in range(counts[ch]):
            row = pl.ds(starts[ch] + j, 1)
            full = pl.ds((starts[ch] + j) * LANES, LANES)
            e = jnp.broadcast_to(states[0, row, :], (SUB, LANES))
            b = jnp.broadcast_to(states[1, row, :], (SUB, LANES))
            for t in range(tiles):
                zs = pl.ds(t * SUB, SUB)
                out[zs, full] = back[zs, full] * (held[zs, full] + b) + reach[zs, full] * e

    w_copy.wait_send()
    for i, ch in order:
        for a in range(2):
            part_copy(i, ch, a).wait_send()
        if i:
            sums_copy(i, ch).wait_send()
    for i in range(1, ks):
        early_copy(i).wait_send()
        for ch in range(chunks):
            late_copy(i, ch).wait_send()


def shards(ys, ks, grad_part, illum_part, source_count, rate, coef_table, coef_index):
    _, rows, lateral = grad_part.shape
    width = lateral // (2 * ys)
    blocks_across = width // LANES
    lead = max(1, blocks_across // 8)
    half = blocks_across // 2
    counts = (lead, half, blocks_across - lead - half)
    chunks, cols = len(counts), half
    cw = cols * LANES
    f32 = jnp.float32
    dma = pltpu.SemaphoreType.DMA
    blocks = (ys, chunks, 2, rows, cw)
    peers = (ys - 1, chunks, 2, rows, cw)
    field = pltpu.VMEM((rows, width), f32)
    anywhere = pl.BlockSpec(memory_space=pl.ANY)
    vmem = pl.BlockSpec(memory_space=pltpu.VMEM)
    return pl.pallas_call(
        functools.partial(body, (ys, ks, rows, width, counts)),
        out_shape=jax.ShapeDtypeStruct((rows, width), f32),
        in_specs=[anywhere, anywhere, vmem, vmem, vmem, vmem],
        out_specs=vmem,
        scratch_shapes=[
            pltpu.VMEM(blocks, f32),
            pltpu.VMEM(blocks, f32),
            pltpu.VMEM(peers, f32),
            pltpu.VMEM(peers, f32),
            pltpu.VMEM((ks, 2, width // LANES, LANES), f32),
            pltpu.VMEM((ks, chunks, 2, cols, LANES), f32),
            field, field, field, field, field,
            pltpu.VMEM((2, width // LANES, LANES), f32),
            pltpu.VMEM((SUB, LANES), f32),
            dma((ys, chunks, 2)),
            dma((ys, chunks, 2)),
            dma((ys, chunks, 2)),
            dma((ys - 1, chunks)),
            dma((ys - 1, chunks)),
            dma((ks - 1,)),
            dma((ks - 1,)),
            dma((ks - 1, chunks)),
            dma((ks - 1, chunks)),
            dma,
            dma,
            pltpu.SemaphoreType.REGULAR((ks // 2 - 1,)),
        ],
        compiler_params=pltpu.CompilerParams(collective_id=0, has_side_effects=True, vmem_limit_bytes=53 * 2**20),
    )(
        grad_part,
        illum_part,
        jnp.broadcast_to(1.0 / source_count.astype(f32)[:, None], (SUB, LANES)),
        rate.reshape(1, -1),
        coef_table.reshape(1, -1),
        coef_index.reshape(1, -1),
    )


def solution(mesh):
    placed = (
        P("shot", "depth", None),
        P("shot", "depth", None),
        P("shot"),
        P("shot"),
        P(),
        P("depth"),
    )
    return jax.shard_map(
        functools.partial(shards, mesh.shape["shot"] // 2, mesh.shape["depth"]),
        mesh=mesh, in_specs=placed, out_specs=P("depth", "shot"), check_vma=False,
    )
```

profile of v0, /device:TPU:0, one launch (start us, length us, event | category | flops | bytes accessed | tf_op | source)
XLA Modules:
  0.0 26.5 jit_solution(3098155463062293381)
XLA Ops:
  0.7 0.0 copy-start
  0.7 0.0 copy-start.1
  0.7 0.0 copy-start.2
  0.7 0.6 %copy-done = f32[2048]{0:T(1024)S(1)} copy-done((f32[2048]{0:T(1024)S(1)}, f32[2048]{0:T(1024)}, u32[]{:S(2)}) %copy-start) | copy-done | bytes 8216
  1.4 0.0 copy-done.1
  1.4 0.0 copy-done.2
  1.4 24.4 %shard_map.64 = f32[32,2048]{1,0:T(8,128)S(1)} custom-call(f32[1,32,8192]{2,1,0:T(8,128)} %grad.1, f32[1,32,8192]{2,1,0:T(8,128)} %illum.1, f32[8,128]{1,0:T(8,128)S(1)} %broadcast_in_dim.9.weight, f32[1,2048]{1,0:T(1,128)S(1)} %bitcast.4, f32[1,64]{1,0:T(1,128)S(1)} %bitcast.5, s32[1,32]{1,0:T(1,128)S(1)} %bitcast.6), custom_call_target="tpu_custom_call" | custom-call | tf_op jit(solution)/shard_map/pallas_call | solution.py:328
  25.8 0.7 %copy.9 = f32[32,2048]{1,0:T(8,128)} copy(f32[32,2048]{1,0:T(8,128)S(1)} %shard_map.64) | data formatting | bytes 524288
  (1 shorter events, 0.0 us)
Async XLA Ops:
  0.7 0.7 %copy-start = (f32[2048]{0:T(1024)S(1)}, f32[2048]{0:T(1024)}, u32[]{:S(2)}) copy-start(f32[2048]{0:T(1024)} %param.9) | copy-start | bytes 24580
  0.7 0.7 %copy-start.1 = (f32[64]{0:T(128)S(1)}, f32[64]{0:T(128)}, u32[]{:S(2)}) copy-start(f32[64]{0:T(128)} %param.10) | copy-start | bytes 772
  0.7 0.7 %copy-start.2 = (s32[32]{0:T(128)S(1)}, s32[32]{0:T(128)}, u32[]{:S(2)}) copy-start(s32[32]{0:T(128)} %param.11) | copy-start | bytes 388
where the time goes:
time: 26.7 us; the launch traced here: 26.5 us
  Pallas kernels  24.4 us (91%)
  local copies, waits for them, and re-layouts  1.36 us (5%)
  between operations  0.73 us (3%)
    pallas_call x1, Pallas kernels, shards(): pl.pallas_call(functools.partial(body, (ys, ks, rows, width, counts)), ou...  24.4 us
    unnamed x7, local copies, waits for them, and re-layouts  1.35 us

commit v1 on v0

v1 whole, which is shorter than its diff:
```python
import functools

import jax
import jax.numpy as jnp
from jax import lax
from jax.experimental import pallas as pl
from jax.experimental.pallas import tpu as pltpu
from jax.sharding import PartitionSpec as P

MESH = pl.DeviceIdType.MESH
LANES = 128
SUB = 8
RELAYS = ()


def body(
    dims,
    grad, illum, count, rate_hbm, table_hbm, index_hbm, out,
    both, sums, landed, early, inject, weigh, back, reach, held, states,
    rate, table, index, mine_count, mate_count, *rest,
):
    ys, ks, rows, width, chunks, sending, taking = dims
    relays = [ch for ch in sending if chunks[ch][2]]
    late, rest = rest[: len(chunks)], rest[len(chunks) :]
    via, rest = dict(zip(relays, rest)), rest[len(relays) :]
    (
        got, part_send, sums_send, sums_recv, via_recv, via_send,
        early_send, early_recv, late_send, late_recv, w_send, w_recv, small_sem, word,
    ) = rest
    tiles = rows // SUB
    me = lax.axis_index("shot")
    d = lax.axis_index("depth")
    y, c = me // 2, me % 2
    mate = y * 2 + 1 - c

    def peer(j):
        return j + (d <= j).astype(jnp.int32)

    def other(i):
        return lax.rem(y + i, ys)

    def greet(semaphore):
        flip = d + 1 - 2 * lax.rem(d, 2)
        pl.semaphore_signal(semaphore, inc=1, device_id=(me, flip), device_id_type=MESH)
        for step in (2, -2):
            near = d + step

            @pl.when((near >= 0) & (near < ks))
            def _():
                pl.semaphore_signal(semaphore, inc=1, device_id=(me, near), device_id_type=MESH)

    def greeted(semaphore, more):
        inner = (d >= 2).astype(jnp.int32) + (d < ks - 2).astype(jnp.int32)
        pl.semaphore_wait(semaphore, inner + 1 + more)

    def relayed(ch, at):
        low, high = chunks[ch][2]
        return (at >= low) & (at < high)

    barrier = pltpu.get_barrier_semaphore()
    pl.semaphore_signal(barrier, inc=1, device_id=(mate, d), device_id_type=MESH)
    for i in range(1, ys):
        pl.semaphore_signal(barrier, inc=1, device_id=(other(i) * 2 + c, d), device_id_type=MESH)
    greet(barrier)
    expected = ys
    if relays:
        expected = expected + (d >= 2).astype(jnp.int32) * (ys - 1)

        @pl.when(d < ks - 2)
        def _():
            for i in range(1, ys):
                pl.semaphore_signal(barrier, inc=1, device_id=(other(i) * 2 + c, d + 2), device_id_type=MESH)

    def columns(ch):
        return pl.ds(chunks[ch][0] * LANES, chunks[ch][1] * LANES)

    def fetch(i, start, cols, semaphore):
        into = pl.ds(i * width + start * LANES, cols * LANES)
        for a, src in enumerate((grad, illum)):
            at = pl.multiple_of((other(i) * 2 + c) * width + start * LANES, LANES)
            pltpu.make_async_copy(
                src.at[0, :, pl.ds(at, cols * LANES)], both.at[0, a, :, into], semaphore
            ).start()

    def give(i, start, cols, semaphore):
        into = pl.ds(i * width + start * LANES, cols * LANES)
        for a, src in enumerate((grad, illum)):
            at = pl.multiple_of((other(i) * 2 + 1 - c) * width + start * LANES, LANES)
            pltpu.make_async_remote_copy(
                src_ref=src.at[0, :, pl.ds(at, cols * LANES)],
                dst_ref=both.at[1, a, :, into],
                send_sem=part_send,
                recv_sem=semaphore,
                device_id=(mate, d),
                device_id_type=MESH,
            ).start()

    def wait_for(ref, semaphore):
        pltpu.make_async_copy(ref, ref, semaphore).wait()

    def arrived(i, start, cols, semaphore):
        wait_for(both.at[:, :, :, pl.ds(i * width + start * LANES, cols * LANES)], semaphore)

    def sums_copy(i, ch):
        return pltpu.make_async_remote_copy(
            src_ref=sums.at[i - 1, :, :, columns(ch)],
            dst_ref=landed.at[i - 1, :, :, columns(ch)],
            send_sem=sums_send,
            recv_sem=sums_recv.at[ch],
            device_id=(other(i) * 2 + c, d),
            device_id_type=MESH,
        )

    def relay_copy(i, ch):
        return pltpu.make_async_remote_copy(
            src_ref=sums.at[i - 1, :, :, columns(ch)],
            dst_ref=via[ch].at[i - 1],
            send_sem=sums_send,
            recv_sem=via_recv.at[relays.index(ch)],
            device_id=(other(i) * 2 + c, d - 2),
            device_id_type=MESH,
        )

    def forward(ch):
        @pl.when(relayed(ch, d + 2))
        def _():
            wait_for(via[ch], via_recv.at[relays.index(ch)])
            for i in range(1, ys):
                pltpu.make_async_remote_copy(
                    src_ref=via[ch].at[i - 1],
                    dst_ref=landed.at[i - 1, :, :, columns(ch)],
                    send_sem=via_send.at[relays.index(ch)],
                    recv_sem=sums_recv.at[ch],
                    device_id=(me, d + 2),
                    device_id_type=MESH,
                ).start()

    def carry_copy(buffer, send, recv, j):
        return pltpu.make_async_remote_copy(
            src_ref=buffer.at[d],
            dst_ref=buffer.at[d],
            send_sem=send,
            recv_sem=recv,
            device_id=(me, peer(j)),
            device_id_type=MESH,
        )

    w_copy = pltpu.make_async_remote_copy(
        src_ref=count,
        dst_ref=mate_count,
        send_sem=w_send,
        recv_sem=w_recv,
        device_id=(mate, d),
        device_id_type=MESH,
    )

    def small_copies():
        pairs = ((count, mine_count), (table_hbm, table), (index_hbm, index), (rate_hbm, rate))
        return [pltpu.make_async_copy(a, b, small_sem.at[n]) for n, (a, b) in enumerate(pairs)]

    first_part = [(i, ch) for ch in sending for i in range(1, ys)]
    for n, (i, ch) in enumerate(first_part):
        fetch(i, *chunks[ch][:2], got.at[n])
    for copy in small_copies():
        copy.start()

    greeted(barrier, expected)
    w_copy.start()
    for n, (i, ch) in enumerate(first_part):
        give(i, *chunks[ch][:2], got.at[n])

    rounds = ks // 2 - 1
    greet(word.at[0])

    def pass_on(r):
        greeted(word.at[r], 0)
        if r + 1 < rounds:
            greet(word.at[r + 1])

    sub = lax.broadcasted_iota(jnp.int32, (SUB, LANES), 0)

    def prefix(v):
        for s in (1, 2, 4):
            v = v + jnp.where(sub >= s, pltpu.roll(v, s, 0), 0.0)
        return v

    def suffix(v):
        for s in (1, 2, 4):
            v = v + jnp.where(sub < SUB - s, pltpu.roll(v, SUB - s, 0), 0.0)
        return v

    def first(v):
        return jnp.broadcast_to(v[0:1], (SUB, LANES))

    def last(v):
        return jnp.broadcast_to(v[SUB - 1 : SUB], (SUB, LANES))

    entries = table.shape[1]

    def upright(row):
        n = row.shape[1]
        diagonal = lax.broadcasted_iota(jnp.int32, (n, n), 0) == lax.broadcasted_iota(
            jnp.int32, (n, n), 1
        )
        return jnp.sum(
            jnp.where(diagonal, jnp.broadcast_to(row, (n, n)), 0.0), axis=1, keepdims=True
        )

    def depths():
        level = lax.broadcasted_iota(jnp.int32, (entries, rows), 0)
        hit = jnp.broadcast_to(index[...], (entries, rows)) == level
        spread = jnp.broadcast_to(upright(table[...]), (entries, rows))
        picked = upright(jnp.sum(jnp.where(hit, spread, 0.0), axis=0, keepdims=True))
        coef, through, before = [], [], []
        total = jnp.zeros((SUB, LANES), jnp.float32)
        for t in range(tiles):
            v = jnp.broadcast_to(picked[t * SUB : (t + 1) * SUB], (SUB, LANES))
            run = prefix(v) + total
            coef.append(v)
            through.append(run)
            before.append(run - v)
            total = last(run)
        return coef, through, before, total

    def terms():
        coef, through, before, total = depths()
        for j in range(width // LANES):
            at = pl.ds(j * LANES, LANES)
            r = jnp.broadcast_to(rate[0:1, at], (SUB, LANES))
            tail = jnp.zeros((SUB, LANES), jnp.float32)
            for t in reversed(range(tiles)):
                zs = pl.ds(t * SUB, SUB)
                rest = 1.0 - jnp.exp(-(coef[t] * r))
                inject[zs, at] = rest * jnp.exp(through[t] * r)
                h = rest * jnp.exp(-((through[t] + before[t]) * r))
                weigh[zs, at] = h
                lift = jnp.exp(before[t] * r)
                back[zs, at] = lift
                run = suffix(h) + tail
                reach[zs, at] = lift * run
                tail = first(run)
            early[d, 0, pl.ds(j, 1), :] = jnp.exp(-(total * r))[0:1]
            early[d, 1, pl.ds(j, 1), :] = tail[0:1]

    copies = small_copies()
    copies[0].wait()
    w_copy.wait_recv()

    def weight(ref):
        return 1.0 / jnp.full((SUB, LANES), ref[0]).astype(jnp.float32)

    w, v = weight(mine_count), weight(mate_count)

    def reduced(i, a, zs, at):
        at = pl.ds(i * width + at.start, at.size)
        if a == 0:
            return both[0, 0, zs, at] * w + both[1, 0, zs, at] * v
        return both[0, 1, zs, at] + both[1, 1, zs, at]

    def lanes(ch):
        return [pl.ds((chunks[ch][0] + j) * LANES, LANES) for j in range(chunks[ch][1])]

    for n, (i, ch) in enumerate(first_part):
        arrived(i, *chunks[ch][:2], got.at[n])
        for at in lanes(ch):
            for t in range(tiles):
                zs = pl.ds(t * SUB, SUB)
                for a in range(2):
                    sums[i - 1, a, zs, at] = reduced(i, a, zs, at)
        if ch in relays:
            pl.when(relayed(ch, d))(relay_copy(i, ch).start)
            pl.when(jnp.logical_not(relayed(ch, d)))(sums_copy(i, ch).start)
        else:
            sums_copy(i, ch).start()
        if n == 0:
            pass_on(0)

    local = len(first_part)
    fetch(0, 0, width // LANES, got.at[local])
    give(0, 0, width // LANES, got.at[local])
    if rounds > 1:
        pass_on(1)
    for copy in copies[1:]:
        copy.wait()
    terms()
    for r in range(2, rounds):
        pass_on(r)
    for j in range(ks - 1):
        carry_copy(early, early_send, early_recv, j).start()

    arrived(0, 0, width // LANES, got.at[local])
    for n, ch in enumerate(taking):
        start, cols, _ = chunks[ch]
        wait_for(landed.at[:, :, :, columns(ch)], sums_recv.at[ch])
        for j, at in enumerate(lanes(ch)):
            carry = jnp.zeros((SUB, LANES), jnp.float32)
            parts = []
            for t in range(tiles):
                zs = pl.ds(t * SUB, SUB)
                num, den = reduced(0, 0, zs, at), reduced(0, 1, zs, at)
                for i in range(1, ys):
                    num = num + landed[i - 1, 0, zs, at]
                    den = den + landed[i - 1, 1, zs, at]
                run = prefix(inject[zs, at] * (num / den)) + carry
                parts.append(run)
                carry = last(run)
            row = pl.ds(start + j, 1)
            late[ch][d, pl.ds(j, 1), :] = carry[0:1] * early[d, 0, row, :]
            tail = jnp.zeros((SUB, LANES), jnp.float32)
            for t in reversed(range(tiles)):
                zs = pl.ds(t * SUB, SUB)
                run = suffix(weigh[zs, at] * parts[t]) + tail
                held[zs, at] = run
                tail = first(run)
            late[ch][d, pl.ds(cols + j, 1), :] = tail[0:1]
        for j in range(ks - 1):
            carry_copy(late[ch], late_send.at[ch], late_recv.at[ch], j).start()
        if n == 0:
            for r in relays:
                forward(r)

    others = pl.ds(0, ks - 1)
    wait_for(early.at[others], early_recv)
    for ch in taking:
        wait_for(late[ch].at[others], late_recv.at[ch])
        start, cols, _ = chunks[ch]
        rs = pl.ds(start, cols)
        down, lift = pl.ds(0, cols), pl.ds(cols, cols)
        state = jnp.zeros((cols, LANES), jnp.float32)
        mine = state
        ups = []
        for k in range(ks):
            mine = jnp.where(k == d, state, mine)
            ups.append(late[ch][k, lift] + early[k, 1, rs] * state)
            if k < ks - 1:
                state = late[ch][k, down] + early[k, 0, rs] * state
        up = jnp.zeros((cols, LANES), jnp.float32)
        for k in reversed(range(1, ks)):
            up = jnp.where(k > d, ups[k] + early[k, 0, rs] * up, up)
        states[0, rs] = mine
        states[1, rs] = up * early[d, 0, rs]
        for j, at in enumerate(lanes(ch)):
            row = pl.ds(start + j, 1)
            e = jnp.broadcast_to(states[0, row, :], (SUB, LANES))
            b = jnp.broadcast_to(states[1, row, :], (SUB, LANES))
            for t in range(tiles):
                zs = pl.ds(t * SUB, SUB)
                out[zs, at] = back[zs, at] * (held[zs, at] + b) + reach[zs, at] * e

    w_copy.wait_send()
    wait_for(both.at[1], part_send)
    wait_for(sums, sums_send)
    for ch in relays:
        pl.when(relayed(ch, d + 2))(
            functools.partial(wait_for, via[ch], via_send.at[relays.index(ch)])
        )
    wait_for(early.at[others], early_send)
    for ch in taking:
        wait_for(late[ch].at[others], late_send.at[ch])


def split(blocks, ys, ks):
    edge = max(1, blocks // 8)
    hops = RELAYS if ys == 2 and ks >= 6 and blocks >= 16 else ()
    inner = blocks - 2 * edge - sum(n for n, _ in hops)
    sizes = [edge, *(n for n, _ in hops), inner - inner // 2, inner // 2, edge]
    ways = [None, *(way(ks) for _, way in hops), None, None, None]
    found = [(sum(sizes[:n]), size, ways[n]) for n, size in enumerate(sizes) if size]
    sending = list(range(len(found)))
    direct = [n for n in sending if not found[n][2]]
    taking = [*direct[:-1], *(n for n in sending if found[n][2]), direct[-1]]
    return found, sending, taking


def shards(ys, ks, grad_part, illum_part, source_count, rate, coef_table, coef_index):
    _, rows, lateral = grad_part.shape
    width = lateral // (2 * ys)
    blocks = width // LANES
    chunks, sending, taking = split(blocks, ys, ks)
    relays = [chunk for chunk in chunks if chunk[2]]
    f32, i32 = jnp.float32, jnp.int32
    dma = pltpu.SemaphoreType.DMA
    sent = pltpu.VMEM((ys - 1, 2, rows, width), f32)
    field = pltpu.VMEM((rows, width), f32)
    anywhere = pl.BlockSpec(memory_space=pl.ANY)
    small = (rate.reshape(1, -1), coef_table.reshape(1, -1), coef_index.reshape(1, -1))
    return pl.pallas_call(
        functools.partial(body, (ys, ks, rows, width, chunks, sending, taking)),
        out_shape=jax.ShapeDtypeStruct((rows, width), f32),
        in_specs=[anywhere] * 6,
        out_specs=pl.BlockSpec(memory_space=pltpu.VMEM),
        scratch_shapes=[
            pltpu.VMEM((2, 2, rows, ys * width), f32),
            sent,
            sent,
            pltpu.VMEM((ks, 2, blocks, LANES), f32),
            field, field, field, field, field,
            pltpu.VMEM((2, blocks, LANES), f32),
            pltpu.VMEM(small[0].shape, f32),
            pltpu.VMEM(small[1].shape, f32),
            pltpu.VMEM(small[2].shape, i32),
            pltpu.SMEM((1,), i32),
            pltpu.SMEM((1,), i32),
            *[pltpu.VMEM((ks, 2 * n, LANES), f32) for _, n, _ in chunks],
            *[pltpu.VMEM((ys - 1, 2, rows, n * LANES), f32) for _, n, _ in relays],
            dma(((ys - 1) * len(chunks) + 1,)),
            dma,
            dma,
            dma((len(chunks),)),
            dma((max(1, len(relays)),)),
            dma((max(1, len(relays)),)),
            dma,
            dma,
            dma((len(chunks),)),
            dma((len(chunks),)),
            dma,
            dma,
            dma((4,)),
            pltpu.SemaphoreType.REGULAR((ks // 2 - 1,)),
        ],
        compiler_params=pltpu.CompilerParams(collective_id=0, has_side_effects=True, vmem_limit_bytes=53 * 2**20),
    )(
        grad_part,
        illum_part,
        source_count,
        *[pltpu.with_memory_space_constraint(x, pltpu.HBM) for x in small],
    )


def solution(mesh):
    placed = (
        P("shot", "depth", None),
        P("shot", "depth", None),
        P("shot"),
        P("shot"),
        P(),
        P("depth"),
    )
    return jax.shard_map(
        functools.partial(shards, mesh.shape["shot"] // 2, mesh.shape["depth"]),
        mesh=mesh, in_specs=placed, out_specs=P("depth", "shot"), check_vma=False,
    )
```

time: 26.7 us -> 25.2 us (0.944)
  Pallas kernels: 24.4 us -> 23.6 us
  local copies, waits for them, and re-layouts: 1.36 us -> 0.71 us
    pallas_call x1, Pallas kernels: 24.4 us -> 23.6 us  [shards(): pl.pallas_call(functools.partial(body, (ys, ks, rows, width, chunks, send...]
    unnamed x7 -> x1, local copies, waits for them, and re-layouts: 1.35 us -> 0.71 us
where the time goes in v1:
time: 25.2 us; the launch traced here: 25 us
  Pallas kernels  23.6 us (94%)
  local copies, waits for them, and re-layouts  0.71 us (3%)
  between operations  0.66 us (3%)
    pallas_call x1, Pallas kernels, shards(): pl.pallas_call(functools.partial(body, (ys, ks, rows, width, chunks, send...  23.6 us
    unnamed x1, local copies, waits for them, and re-layouts  0.71 us

profile of v1, /device:TPU:0, one launch (start us, length us, event | category | flops | bytes accessed | tf_op | source)
XLA Modules:
  0.0 25.0 jit_solution(14820712692564545515)
XLA Ops:
  0.7 23.6 %shard_map.64 = f32[32,2048]{1,0:T(8,128)S(1)} custom-call(f32[1,32,8192]{2,1,0:T(8,128)} %grad.1, f32[1,32,8192]{2,1,0:T(8,128)} %illum.1, s32[1]{0:T(128)S(6)} %copy.8.count, f32[1,2048]{1,0:T(1,128)} %bitcast.3, f32[1,64]{1,0:T(1,128)} %bitcast.4, s32[1,32]{1,0:T(1,128)} %bitcast.5), custom_call_target="tpu_custom_call" | custom-call | tf_op jit(solution)/shard_map/pallas_call | solution.py:387
  24.3 0.7 %copy.9 = f32[32,2048]{1,0:T(8,128)} copy(f32[32,2048]{1,0:T(8,128)S(1)} %shard_map.64) | data formatting | bytes 524288

commit v2 on v1

--- a/solution.py
+++ b/solution.py
@@ -10,7 +10,7 @@
 MESH = pl.DeviceIdType.MESH
 LANES = 128
 SUB = 8
-RELAYS = ()
+RELAYS = ((2, lambda ks: (2, ks)), (1, lambda ks: (ks - 4, ks - 2)))
 
 
 def body(

time: 25.2 us -> 24.5 us (0.972)
  Pallas kernels: 23.6 us -> 22.9 us
    pallas_call x1, Pallas kernels: 23.6 us -> 22.9 us  [shards(): pl.pallas_call(functools.partial(body, (ys, ks, rows, width, chunks, send...]
where the time goes in v2:
time: 24.5 us; the launch traced here: 24.3 us
  Pallas kernels  22.9 us (93%)
  local copies, waits for them, and re-layouts  0.71 us (3%)
  between operations  0.66 us (3%)
    pallas_call x1, Pallas kernels, shards(): pl.pallas_call(functools.partial(body, (ys, ks, rows, width, chunks, send...  22.9 us
    unnamed x1, local copies, waits for them, and re-layouts  0.71 us

profile of v2, /device:TPU:0, one launch (start us, length us, event | category | flops | bytes accessed | tf_op | source)
XLA Modules:
  0.0 24.3 jit_solution(17725055376853016525)
XLA Ops:
  0.7 22.9 %shard_map.64 = f32[32,2048]{1,0:T(8,128)S(1)} custom-call(f32[1,32,8192]{2,1,0:T(8,128)} %grad.1, f32[1,32,8192]{2,1,0:T(8,128)} %illum.1, s32[1]{0:T(128)S(6)} %copy.8.count, f32[1,2048]{1,0:T(1,128)} %bitcast.3, f32[1,64]{1,0:T(1,128)} %bitcast.4, s32[1,32]{1,0:T(1,128)} %bitcast.5), custom_call_target="tpu_custom_call" | custom-call | tf_op jit(solution)/shard_map/pallas_call | solution.py:387
  23.6 0.7 %copy.9 = f32[32,2048]{1,0:T(8,128)} copy(f32[32,2048]{1,0:T(8,128)S(1)} %shard_map.64) | data formatting | bytes 524288

commit v3 on v2

--- a/solution.py
+++ b/solution.py
@@ -10,7 +10,22 @@
 MESH = pl.DeviceIdType.MESH
 LANES = 128
 SUB = 8
-RELAYS = ((2, lambda ks: (2, ks)), (1, lambda ks: (ks - 4, ks - 2)))
+
+
+def deep(at, ks):
+    return (at >= 2) & (at < ks)
+
+
+def middle(at, ks):
+    return (at >= ks - 4) & (at < ks - 2)
+
+
+def odd(at, ks):
+    return lax.rem(at, 2) == 1
+
+
+ROUTES = ((2, deep), (1, odd))
+RELAYS = ((2, (2, deep)), (1, (2, middle)), (1, (1, odd)))
 
 
 def body(
@@ -49,27 +64,28 @@
             def _():
                 pl.semaphore_signal(semaphore, inc=1, device_id=(me, near), device_id_type=MESH)
 
-    def greeted(semaphore, more):
-        inner = (d >= 2).astype(jnp.int32) + (d < ks - 2).astype(jnp.int32)
-        pl.semaphore_wait(semaphore, inner + 1 + more)
+    def neighbours():
+        return (d >= 2).astype(jnp.int32) + (d < ks - 2).astype(jnp.int32) + 1
 
     def relayed(ch, at):
-        low, high = chunks[ch][2]
-        return (at >= low) & (at < high)
+        return chunks[ch][2][1](at, ks)
+
+    def stride(ch):
+        return chunks[ch][2][0]
 
     barrier = pltpu.get_barrier_semaphore()
     pl.semaphore_signal(barrier, inc=1, device_id=(mate, d), device_id_type=MESH)
     for i in range(1, ys):
         pl.semaphore_signal(barrier, inc=1, device_id=(other(i) * 2 + c, d), device_id_type=MESH)
-    greet(barrier)
-    expected = ys
-    if relays:
-        expected = expected + (d >= 2).astype(jnp.int32) * (ys - 1)
-
-        @pl.when(d < ks - 2)
+    pl.when(y == 0)(functools.partial(greet, barrier))
+    expected = ys + (y == 0).astype(jnp.int32) * neighbours()
+    for step, some in ROUTES if relays else ():
+        expected = expected + some(d, ks).astype(jnp.int32) * (ys - 1)
+
+        @pl.when(some(d + step, ks))
         def _():
             for i in range(1, ys):
-                pl.semaphore_signal(barrier, inc=1, device_id=(other(i) * 2 + c, d + 2), device_id_type=MESH)
+                pl.semaphore_signal(barrier, inc=1, device_id=(other(i) * 2 + c, d + step), device_id_type=MESH)
 
     def columns(ch):
         return pl.ds(chunks[ch][0] * LANES, chunks[ch][1] * LANES)
@@ -117,12 +133,12 @@
             dst_ref=via[ch].at[i - 1],
             send_sem=sums_send,
             recv_sem=via_recv.at[relays.index(ch)],
-            device_id=(other(i) * 2 + c, d - 2),
+            device_id=(other(i) * 2 + c, d - stride(ch)),
             device_id_type=MESH,
         )
 
     def forward(ch):
-        @pl.when(relayed(ch, d + 2))
+        @pl.when(relayed(ch, d + stride(ch)))
         def _():
             wait_for(via[ch], via_recv.at[relays.index(ch)])
             for i in range(1, ys):
@@ -131,7 +147,7 @@
                     dst_ref=landed.at[i - 1, :, :, columns(ch)],
                     send_sem=via_send.at[relays.index(ch)],
                     recv_sem=sums_recv.at[ch],
-                    device_id=(me, d + 2),
+                    device_id=(me, d + stride(ch)),
                     device_id_type=MESH,
                 ).start()
 
@@ -164,18 +180,28 @@
     for copy in small_copies():
         copy.start()
 
-    greeted(barrier, expected)
+    pl.semaphore_wait(barrier, expected)
     w_copy.start()
     for n, (i, ch) in enumerate(first_part):
         give(i, *chunks[ch][:2], got.at[n])
 
-    rounds = ks // 2 - 1
-    greet(word.at[0])
+    rounds = ks // 2
+    pl.when(y == 0)(functools.partial(greet, word.at[0]))
 
     def pass_on(r):
-        greeted(word.at[r], 0)
-        if r + 1 < rounds:
-            greet(word.at[r + 1])
+        @pl.when(y == 0)
+        def _():
+            pl.semaphore_wait(word.at[r], neighbours())
+            if r + 1 < rounds:
+                greet(word.at[r + 1])
+            else:
+                for i in range(1, ys):
+                    pl.semaphore_signal(
+                        word.at[rounds], inc=1, device_id=(other(i) * 2 + c, d), device_id_type=MESH
+                    )
+
+        if r + 1 == rounds:
+            pl.when(y != 0)(lambda: pl.semaphore_wait(word.at[rounds], 1))
 
     sub = lax.broadcasted_iota(jnp.int32, (SUB, LANES), 0)
 
@@ -351,7 +377,7 @@
     wait_for(both.at[1], part_send)
     wait_for(sums, sums_send)
     for ch in relays:
-        pl.when(relayed(ch, d + 2))(
+        pl.when(relayed(ch, d + stride(ch)))(
             functools.partial(wait_for, via[ch], via_send.at[relays.index(ch)])
         )
     wait_for(early.at[others], early_send)
@@ -364,7 +390,7 @@
     hops = RELAYS if ys == 2 and ks >= 6 and blocks >= 16 else ()
     inner = blocks - 2 * edge - sum(n for n, _ in hops)
     sizes = [edge, *(n for n, _ in hops), inner - inner // 2, inner // 2, edge]
-    ways = [None, *(way(ks) for _, way in hops), None, None, None]
+    ways = [None, *(way for _, way in hops), None, None, None]
     found = [(sum(sizes[:n]), size, ways[n]) for n, size in enumerate(sizes) if size]
     sending = list(range(len(found)))
     direct = [n for n in sending if not found[n][2]]
@@ -416,7 +442,7 @@
             dma,
             dma,
             dma((4,)),
-            pltpu.SemaphoreType.REGULAR((ks // 2 - 1,)),
+            pltpu.SemaphoreType.REGULAR((ks // 2 + 1,)),
         ],
         compiler_params=pltpu.CompilerParams(collective_id=0, has_side_effects=True, vmem_limit_bytes=53 * 2**20),
     )(

time: 24.5 us -> 23.7 us (0.967)
  Pallas kernels: 22.9 us -> 22.2 us
    pallas_call x1, Pallas kernels: 22.9 us -> 22.2 us  [shards(): pl.pallas_call(functools.partial(body, (ys, ks, rows, width, chunks, send...]
where the time goes in v3:
time: 23.7 us; the launch traced here: 23.6 us
  Pallas kernels  22.2 us (94%)
  local copies, waits for them, and re-layouts  0.71 us (3%)
  between operations  0.66 us (3%)
    pallas_call x1, Pallas kernels, shards(): pl.pallas_call(functools.partial(body, (ys, ks, rows, width, chunks, send...  22.2 us
    unnamed x1, local copies, waits for them, and re-layouts  0.71 us

profile of v3, /device:TPU:0, one launch (start us, length us, event | category | flops | bytes accessed | tf_op | source)
XLA Modules:
  0.0 23.6 jit_solution(16670962413417967737)
XLA Ops:
  0.7 22.2 %shard_map.64 = f32[32,2048]{1,0:T(8,128)S(1)} custom-call(f32[1,32,8192]{2,1,0:T(8,128)} %grad.1, f32[1,32,8192]{2,1,0:T(8,128)} %illum.1, s32[1]{0:T(128)S(6)} %copy.8.count, f32[1,2048]{1,0:T(1,128)} %bitcast.3, f32[1,64]{1,0:T(1,128)} %bitcast.4, s32[1,32]{1,0:T(1,128)} %bitcast.5), custom_call_target="tpu_custom_call" | custom-call | tf_op jit(solution)/shard_map/pallas_call | solution.py:413
  22.9 0.7 %copy.9 = f32[32,2048]{1,0:T(8,128)} copy(f32[32,2048]{1,0:T(8,128)S(1)} %shard_map.64) | data formatting | bytes 524288

commit v4 on v3

--- a/solution.py
+++ b/solution.py
@@ -268,7 +268,19 @@
             early[d, 0, pl.ds(j, 1), :] = jnp.exp(-(total * r))[0:1]
             early[d, 1, pl.ds(j, 1), :] = tail[0:1]
 
+    def prepare():
+        for copy in copies[1:]:
+            copy.wait()
+        terms()
+
+    turn = word.at[rounds + 1]
     copies = small_copies()
+
+    @pl.when(c == 1)
+    def _():
+        prepare()
+        pl.semaphore_wait(turn, 1)
+
     copies[0].wait()
     w_copy.wait_recv()
 
@@ -298,18 +310,17 @@
             pl.when(jnp.logical_not(relayed(ch, d)))(sums_copy(i, ch).start)
         else:
             sums_copy(i, ch).start()
-        if n == 0:
-            pass_on(0)
 
     local = len(first_part)
     fetch(0, 0, width // LANES, got.at[local])
     give(0, 0, width // LANES, got.at[local])
-    if rounds > 1:
-        pass_on(1)
-    for copy in copies[1:]:
-        copy.wait()
-    terms()
-    for r in range(2, rounds):
+
+    @pl.when(c == 0)
+    def _():
+        prepare()
+        pl.semaphore_signal(turn, inc=1, device_id=(mate, d), device_id_type=MESH)
+
+    for r in range(rounds):
         pass_on(r)
     for j in range(ks - 1):
         carry_copy(early, early_send, early_recv, j).start()
@@ -391,11 +402,10 @@
     inner = blocks - 2 * edge - sum(n for n, _ in hops)
     sizes = [edge, *(n for n, _ in hops), inner - inner // 2, inner // 2, edge]
     ways = [None, *(way for _, way in hops), None, None, None]
-    found = [(sum(sizes[:n]), size, ways[n]) for n, size in enumerate(sizes) if size]
-    sending = list(range(len(found)))
-    direct = [n for n in sending if not found[n][2]]
-    taking = [*direct[:-1], *(n for n in sending if found[n][2]), direct[-1]]
-    return found, sending, taking
+    found = [(sum(sizes[:n]), size, ways[n]) for n, size in enumerate(sizes)]
+    detours = range(1, len(hops) + 1)
+    straight = range(len(hops) + 1, len(found) - 1)
+    return found, range(len(found)), [0, *straight, *detours, len(found) - 1]
 
 
 def shards(ys, ks, grad_part, illum_part, source_count, rate, coef_table, coef_index):
@@ -442,7 +452,7 @@
             dma,
             dma,
             dma((4,)),
-            pltpu.SemaphoreType.REGULAR((ks // 2 + 1,)),
+            pltpu.SemaphoreType.REGULAR((ks // 2 + 2,)),
         ],
         compiler_params=pltpu.CompilerParams(collective_id=0, has_side_effects=True, vmem_limit_bytes=53 * 2**20),
     )(

time: 23.7 us -> 23 us (0.970)
  Pallas kernels: 22.2 us -> 21.5 us
    pallas_call x1, Pallas kernels: 22.2 us -> 21.5 us  [shards(): pl.pallas_call(functools.partial(body, (ys, ks, rows, width, chunks, send...]
where the time goes in v4:
time: 23 us; the launch traced here: 22.8 us
  Pallas kernels  21.5 us (93%)
  local copies, waits for them, and re-layouts  0.71 us (3%)
  between operations  0.66 us (3%)
    pallas_call x1, Pallas kernels, shards(): pl.pallas_call(functools.partial(body, (ys, ks, rows, width, chunks, send...  21.5 us
    unnamed x1, local copies, waits for them, and re-layouts  0.71 us

profile of v4, /device:TPU:0, one launch (start us, length us, event | category | flops | bytes accessed | tf_op | source)
XLA Modules:
  0.0 22.8 jit_solution(6852820266141446117)
XLA Ops:
  0.7 21.5 %shard_map.64 = f32[32,2048]{1,0:T(8,128)S(1)} custom-call(f32[1,32,8192]{2,1,0:T(8,128)} %grad.1, f32[1,32,8192]{2,1,0:T(8,128)} %illum.1, s32[1]{0:T(128)S(6)} %copy.8.count, f32[1,2048]{1,0:T(1,128)} %bitcast.3, f32[1,64]{1,0:T(1,128)} %bitcast.4, s32[1,32]{1,0:T(1,128)} %bitcast.5), custom_call_target="tpu_custom_call" | custom-call | tf_op jit(solution)/shard_map/pallas_call | solution.py:423
  22.1 0.7 %copy.9 = f32[32,2048]{1,0:T(8,128)} copy(f32[32,2048]{1,0:T(8,128)S(1)} %shard_map.64) | data formatting | bytes 524288

commit v5 on v4

--- a/solution.py
+++ b/solution.py
@@ -17,7 +17,7 @@
 
 
 def middle(at, ks):
-    return (at >= ks - 4) & (at < ks - 2)
+    return (at >= 2) & (at < ks - 2)
 
 
 def odd(at, ks):
@@ -32,11 +32,11 @@
     dims,
     grad, illum, count, rate_hbm, table_hbm, index_hbm, out,
     both, sums, landed, early, inject, weigh, back, reach, held, states,
-    rate, table, index, mine_count, mate_count, *rest,
+    rate, table, index, mate_count, *rest,
 ):
-    ys, ks, rows, width, chunks, sending, taking = dims
-    relays = [ch for ch in sending if chunks[ch][2]]
-    late, rest = rest[: len(chunks)], rest[len(chunks) :]
+    ys, ks, rows, width, chunks, loads, turns = dims
+    relays = [ch for ch in range(len(chunks)) if chunks[ch][2]]
+    late, rest = rest[: len(turns)], rest[len(turns) :]
     via, rest = dict(zip(relays, rest)), rest[len(relays) :]
     (
         got, part_send, sums_send, sums_recv, via_recv, via_send,
@@ -86,6 +86,9 @@
         def _():
             for i in range(1, ys):
                 pl.semaphore_signal(barrier, inc=1, device_id=(other(i) * 2 + c, d + step), device_id_type=MESH)
+
+    def reach_of(group):
+        return chunks[group[0]][0], sum(chunks[ch][1] for ch in group)
 
     def columns(ch):
         return pl.ds(chunks[ch][0] * LANES, chunks[ch][1] * LANES)
@@ -171,19 +174,20 @@
     )
 
     def small_copies():
-        pairs = ((count, mine_count), (table_hbm, table), (index_hbm, index), (rate_hbm, rate))
+        pairs = ((table_hbm, table), (index_hbm, index), (rate_hbm, rate))
         return [pltpu.make_async_copy(a, b, small_sem.at[n]) for n, (a, b) in enumerate(pairs)]
 
-    first_part = [(i, ch) for ch in sending for i in range(1, ys)]
-    for n, (i, ch) in enumerate(first_part):
-        fetch(i, *chunks[ch][:2], got.at[n])
+    first_part = [(i, group) for group in loads for i in range(1, ys)]
+    fetch(1, *reach_of(loads[0]), got.at[0])
+
+    pl.semaphore_wait(barrier, expected)
+    w_copy.start()
+    for n, (i, group) in enumerate(first_part):
+        give(i, *reach_of(group), got.at[n])
+    for n, (i, group) in enumerate(first_part[1:], 1):
+        fetch(i, *reach_of(group), got.at[n])
     for copy in small_copies():
         copy.start()
-
-    pl.semaphore_wait(barrier, expected)
-    w_copy.start()
-    for n, (i, ch) in enumerate(first_part):
-        give(i, *chunks[ch][:2], got.at[n])
 
     rounds = ks // 2
     pl.when(y == 0)(functools.partial(greet, word.at[0]))
@@ -269,25 +273,23 @@
             early[d, 1, pl.ds(j, 1), :] = tail[0:1]
 
     def prepare():
-        for copy in copies[1:]:
+        for copy in small_copies():
             copy.wait()
         terms()
 
     turn = word.at[rounds + 1]
-    copies = small_copies()
 
     @pl.when(c == 1)
     def _():
         prepare()
         pl.semaphore_wait(turn, 1)
 
-    copies[0].wait()
     w_copy.wait_recv()
 
     def weight(ref):
         return 1.0 / jnp.full((SUB, LANES), ref[0]).astype(jnp.float32)
 
-    w, v = weight(mine_count), weight(mate_count)
+    w, v = weight(count), weight(mate_count)
 
     def reduced(i, a, zs, at):
         at = pl.ds(i * width + at.start, at.size)
@@ -295,21 +297,22 @@
             return both[0, 0, zs, at] * w + both[1, 0, zs, at] * v
         return both[0, 1, zs, at] + both[1, 1, zs, at]
 
-    def lanes(ch):
-        return [pl.ds((chunks[ch][0] + j) * LANES, LANES) for j in range(chunks[ch][1])]
-
-    for n, (i, ch) in enumerate(first_part):
-        arrived(i, *chunks[ch][:2], got.at[n])
-        for at in lanes(ch):
-            for t in range(tiles):
-                zs = pl.ds(t * SUB, SUB)
-                for a in range(2):
-                    sums[i - 1, a, zs, at] = reduced(i, a, zs, at)
-        if ch in relays:
-            pl.when(relayed(ch, d))(relay_copy(i, ch).start)
-            pl.when(jnp.logical_not(relayed(ch, d)))(sums_copy(i, ch).start)
-        else:
-            sums_copy(i, ch).start()
+    def lanes(start, cols):
+        return [pl.ds((start + j) * LANES, LANES) for j in range(cols)]
+
+    for n, (i, group) in enumerate(first_part):
+        arrived(i, *reach_of(group), got.at[n])
+        for ch in group:
+            for at in lanes(*chunks[ch][:2]):
+                for t in range(tiles):
+                    zs = pl.ds(t * SUB, SUB)
+                    for a in range(2):
+                        sums[i - 1, a, zs, at] = reduced(i, a, zs, at)
+            if ch in relays:
+                pl.when(relayed(ch, d))(relay_copy(i, ch).start)
+                pl.when(jnp.logical_not(relayed(ch, d)))(sums_copy(i, ch).start)
+            else:
+                sums_copy(i, ch).start()
 
     local = len(first_part)
     fetch(0, 0, width // LANES, got.at[local])
@@ -326,10 +329,11 @@
         carry_copy(early, early_send, early_recv, j).start()
 
     arrived(0, 0, width // LANES, got.at[local])
-    for n, ch in enumerate(taking):
-        start, cols, _ = chunks[ch]
-        wait_for(landed.at[:, :, :, columns(ch)], sums_recv.at[ch])
-        for j, at in enumerate(lanes(ch)):
+    for n, group in enumerate(turns):
+        start, cols = reach_of(group)
+        for ch in group:
+            wait_for(landed.at[:, :, :, columns(ch)], sums_recv.at[ch])
+        for j, at in enumerate(lanes(start, cols)):
             carry = jnp.zeros((SUB, LANES), jnp.float32)
             parts = []
             for t in range(tiles):
@@ -342,25 +346,25 @@
                 parts.append(run)
                 carry = last(run)
             row = pl.ds(start + j, 1)
-            late[ch][d, pl.ds(j, 1), :] = carry[0:1] * early[d, 0, row, :]
+            late[n][d, pl.ds(j, 1), :] = carry[0:1] * early[d, 0, row, :]
             tail = jnp.zeros((SUB, LANES), jnp.float32)
             for t in reversed(range(tiles)):
                 zs = pl.ds(t * SUB, SUB)
                 run = suffix(weigh[zs, at] * parts[t]) + tail
                 held[zs, at] = run
                 tail = first(run)
-            late[ch][d, pl.ds(cols + j, 1), :] = tail[0:1]
+            late[n][d, pl.ds(cols + j, 1), :] = tail[0:1]
         for j in range(ks - 1):
-            carry_copy(late[ch], late_send.at[ch], late_recv.at[ch], j).start()
+            carry_copy(late[n], late_send, late_recv.at[n], j).start()
         if n == 0:
             for r in relays:
                 forward(r)
 
     others = pl.ds(0, ks - 1)
     wait_for(early.at[others], early_recv)
-    for ch in taking:
-        wait_for(late[ch].at[others], late_recv.at[ch])
-        start, cols, _ = chunks[ch]
+    for n, group in enumerate(turns):
+        wait_for(late[n].at[others], late_recv.at[n])
+        start, cols = reach_of(group)
         rs = pl.ds(start, cols)
         down, lift = pl.ds(0, cols), pl.ds(cols, cols)
         state = jnp.zeros((cols, LANES), jnp.float32)
@@ -368,15 +372,15 @@
         ups = []
         for k in range(ks):
             mine = jnp.where(k == d, state, mine)
-            ups.append(late[ch][k, lift] + early[k, 1, rs] * state)
+            ups.append(late[n][k, lift] + early[k, 1, rs] * state)
             if k < ks - 1:
-                state = late[ch][k, down] + early[k, 0, rs] * state
+                state = late[n][k, down] + early[k, 0, rs] * state
         up = jnp.zeros((cols, LANES), jnp.float32)
         for k in reversed(range(1, ks)):
             up = jnp.where(k > d, ups[k] + early[k, 0, rs] * up, up)
         states[0, rs] = mine
         states[1, rs] = up * early[d, 0, rs]
-        for j, at in enumerate(lanes(ch)):
+        for j, at in enumerate(lanes(start, cols)):
             row = pl.ds(start + j, 1)
             e = jnp.broadcast_to(states[0, row, :], (SUB, LANES))
             b = jnp.broadcast_to(states[1, row, :], (SUB, LANES))
@@ -392,27 +396,26 @@
             functools.partial(wait_for, via[ch], via_send.at[relays.index(ch)])
         )
     wait_for(early.at[others], early_send)
-    for ch in taking:
-        wait_for(late[ch].at[others], late_send.at[ch])
+    wait_for(early.at[others], late_send)
 
 
 def split(blocks, ys, ks):
     edge = max(1, blocks // 8)
     hops = RELAYS if ys == 2 and ks >= 6 and blocks >= 16 else ()
     inner = blocks - 2 * edge - sum(n for n, _ in hops)
-    sizes = [edge, *(n for n, _ in hops), inner - inner // 2, inner // 2, edge]
+    sizes = [max(1, edge // 2), *(n for n, _ in hops), inner - inner // 2, inner // 2 + edge - max(1, edge // 2), edge]
     ways = [None, *(way for _, way in hops), None, None, None]
     found = [(sum(sizes[:n]), size, ways[n]) for n, size in enumerate(sizes)]
-    detours = range(1, len(hops) + 1)
-    straight = range(len(hops) + 1, len(found) - 1)
-    return found, range(len(found)), [0, *straight, *detours, len(found) - 1]
+    n = len(hops) + 1
+    detours = [tuple(range(1, n))] if hops else []
+    return found, [(0,), *detours, (n, n + 1, n + 2)], [(0,), (n,), (n + 1,), *[(m,) for m in range(1, n)], (n + 2,)]
 
 
 def shards(ys, ks, grad_part, illum_part, source_count, rate, coef_table, coef_index):
     _, rows, lateral = grad_part.shape
     width = lateral // (2 * ys)
     blocks = width // LANES
-    chunks, sending, taking = split(blocks, ys, ks)
+    chunks, loads, turns = split(blocks, ys, ks)
     relays = [chunk for chunk in chunks if chunk[2]]
     f32, i32 = jnp.float32, jnp.int32
     dma = pltpu.SemaphoreType.DMA
@@ -421,9 +424,9 @@
     anywhere = pl.BlockSpec(memory_space=pl.ANY)
     small = (rate.reshape(1, -1), coef_table.reshape(1, -1), coef_index.reshape(1, -1))
     return pl.pallas_call(
-        functools.partial(body, (ys, ks, rows, width, chunks, sending, taking)),
+        functools.partial(body, (ys, ks, rows, width, chunks, loads, turns)),
         out_shape=jax.ShapeDtypeStruct((rows, width), f32),
-        in_specs=[anywhere] * 6,
+        in_specs=[anywhere] * 2 + [pl.BlockSpec(memory_space=pltpu.SMEM)] + [anywhere] * 3,
         out_specs=pl.BlockSpec(memory_space=pltpu.VMEM),
         scratch_shapes=[
             pltpu.VMEM((2, 2, rows, ys * width), f32),
@@ -436,10 +439,9 @@
             pltpu.VMEM(small[1].shape, f32),
             pltpu.VMEM(small[2].shape, i32),
             pltpu.SMEM((1,), i32),
-            pltpu.SMEM((1,), i32),
-            *[pltpu.VMEM((ks, 2 * n, LANES), f32) for _, n, _ in chunks],
+            *[pltpu.VMEM((ks, 2 * sum(chunks[ch][1] for ch in group), LANES), f32) for group in turns],
             *[pltpu.VMEM((ys - 1, 2, rows, n * LANES), f32) for _, n, _ in relays],
-            dma(((ys - 1) * len(chunks) + 1,)),
+            dma(((ys - 1) * len(loads) + 1,)),
             dma,
             dma,
             dma((len(chunks),)),
@@ -447,11 +449,11 @@
             dma((max(1, len(relays)),)),
             dma,
             dma,
-            dma((len(chunks),)),
-            dma((len(chunks),)),
-            dma,
-            dma,
-            dma((4,)),
+            dma,
+            dma((len(turns),)),
+            dma,
+            dma,
+            dma((3,)),
             pltpu.SemaphoreType.REGULAR((ks // 2 + 2,)),
         ],
         compiler_params=pltpu.CompilerParams(collective_id=0, has_side_effects=True, vmem_limit_bytes=53 * 2**20),

time: 23 us -> 22.7 us (0.987)
  Pallas kernels: 21.5 us -> 21.2 us
    pallas_call x1, Pallas kernels: 21.5 us -> 21.2 us  [shards(): pl.pallas_call(functools.partial(body, (ys, ks, rows, width, chunks, load...]
where the time goes in v5:
time: 22.7 us; the launch traced here: 22.5 us
  Pallas kernels  21.2 us (93%)
  local copies, waits for them, and re-layouts  0.71 us (3%)
  between operations  0.66 us (3%)
    pallas_call x1, Pallas kernels, shards(): pl.pallas_call(functools.partial(body, (ys, ks, rows, width, chunks, load...  21.2 us
    unnamed x1, local copies, waits for them, and re-layouts  0.71 us

profile of v5, /device:TPU:0, one launch (start us, length us, event | category | flops | bytes accessed | tf_op | source)
XLA Modules:
  0.0 22.5 jit_solution(12783521543870541803)
XLA Ops:
  0.7 21.2 %shard_map.64 = f32[32,2048]{1,0:T(8,128)S(1)} custom-call(f32[1,32,8192]{2,1,0:T(8,128)} %grad.1, f32[1,32,8192]{2,1,0:T(8,128)} %illum.1, s32[1]{0:T(128)S(6)} %copy.8.count, f32[1,2048]{1,0:T(1,128)} %bitcast.3, f32[1,64]{1,0:T(1,128)} %bitcast.4, s32[1,32]{1,0:T(1,128)} %bitcast.5), custom_call_target="tpu_custom_call" | custom-call | tf_op jit(solution)/shard_map/pallas_call | solution.py:426
  21.8 0.7 %copy.9 = f32[32,2048]{1,0:T(8,128)} copy(f32[32,2048]{1,0:T(8,128)S(1)} %shard_map.64) | data formatting | bytes 524288

commit v6 on v5

--- a/solution.py
+++ b/solution.py
@@ -82,10 +82,13 @@
     for step, some in ROUTES if relays else ():
         expected = expected + some(d, ks).astype(jnp.int32) * (ys - 1)
 
-        @pl.when(some(d + step, ks))
+        @pl.when((c == 1) & some(d + step, ks))
         def _():
             for i in range(1, ys):
-                pl.semaphore_signal(barrier, inc=1, device_id=(other(i) * 2 + c, d + step), device_id_type=MESH)
+                for own in range(2):
+                    pl.semaphore_signal(
+                        barrier, inc=1, device_id=(other(i) * 2 + own, d + step), device_id_type=MESH
+                    )
 
     def reach_of(group):
         return chunks[group[0]][0], sum(chunks[ch][1] for ch in group)
@@ -133,26 +136,30 @@
     def relay_copy(i, ch):
         return pltpu.make_async_remote_copy(
             src_ref=sums.at[i - 1, :, :, columns(ch)],
-            dst_ref=via[ch].at[i - 1],
+            dst_ref=via[ch].at[c, i - 1],
             send_sem=sums_send,
-            recv_sem=via_recv.at[relays.index(ch)],
-            device_id=(other(i) * 2 + c, d - stride(ch)),
+            recv_sem=via_recv.at[c, relays.index(ch)],
+            device_id=(other(i) * 2 + 1, d - stride(ch)),
             device_id_type=MESH,
         )
 
+    def forwards(ch):
+        return (c == 1) & relayed(ch, d + stride(ch))
+
     def forward(ch):
-        @pl.when(relayed(ch, d + stride(ch)))
+        @pl.when(forwards(ch))
         def _():
-            wait_for(via[ch], via_recv.at[relays.index(ch)])
-            for i in range(1, ys):
-                pltpu.make_async_remote_copy(
-                    src_ref=via[ch].at[i - 1],
-                    dst_ref=landed.at[i - 1, :, :, columns(ch)],
-                    send_sem=via_send.at[relays.index(ch)],
-                    recv_sem=sums_recv.at[ch],
-                    device_id=(me, d + stride(ch)),
-                    device_id_type=MESH,
-                ).start()
+            for own in range(2):
+                wait_for(via[ch].at[own], via_recv.at[own, relays.index(ch)])
+                for i in range(1, ys):
+                    pltpu.make_async_remote_copy(
+                        src_ref=via[ch].at[own, i - 1],
+                        dst_ref=landed.at[i - 1, :, :, columns(ch)],
+                        send_sem=via_send.at[relays.index(ch)],
+                        recv_sem=sums_recv.at[ch],
+                        device_id=(y * 2 + own, d + stride(ch)),
+                        device_id_type=MESH,
+                    ).start()
 
     def carry_copy(buffer, send, recv, j):
         return pltpu.make_async_remote_copy(
@@ -325,6 +332,8 @@
 
     for r in range(rounds):
         pass_on(r)
+    for r in relays:
+        forward(r)
     for j in range(ks - 1):
         carry_copy(early, early_send, early_recv, j).start()
 
@@ -356,9 +365,6 @@
             late[n][d, pl.ds(cols + j, 1), :] = tail[0:1]
         for j in range(ks - 1):
             carry_copy(late[n], late_send, late_recv.at[n], j).start()
-        if n == 0:
-            for r in relays:
-                forward(r)
 
     others = pl.ds(0, ks - 1)
     wait_for(early.at[others], early_recv)
@@ -392,7 +398,7 @@
     wait_for(both.at[1], part_send)
     wait_for(sums, sums_send)
     for ch in relays:
-        pl.when(relayed(ch, d + stride(ch)))(
+        pl.when(forwards(ch))(
             functools.partial(wait_for, via[ch], via_send.at[relays.index(ch)])
         )
     wait_for(early.at[others], early_send)
@@ -440,12 +446,12 @@
             pltpu.VMEM(small[2].shape, i32),
             pltpu.SMEM((1,), i32),
             *[pltpu.VMEM((ks, 2 * sum(chunks[ch][1] for ch in group), LANES), f32) for group in turns],
-            *[pltpu.VMEM((ys - 1, 2, rows, n * LANES), f32) for _, n, _ in relays],
+            *[pltpu.VMEM((2, ys - 1, 2, rows, n * LANES), f32) for _, n, _ in relays],
             dma(((ys - 1) * len(loads) + 1,)),
             dma,
             dma,
             dma((len(chunks),)),
-            dma((max(1, len(relays)),)),
+            dma((2, max(1, len(relays)))),
             dma((max(1, len(relays)),)),
             dma,
             dma,

time: 22.7 us -> 22.7 us (level)
  no operation moved by 1% of the time
where the time goes in v6:
time: 22.7 us; the launch traced here: 22.5 us
  Pallas kernels  21.2 us (93%)
  local copies, waits for them, and re-layouts  0.71 us (3%)
  between operations  0.66 us (3%)
    pallas_call x1, Pallas kernels, shards(): pl.pallas_call(functools.partial(body, (ys, ks, rows, width, chunks, load...  21.2 us
    unnamed x1, local copies, waits for them, and re-layouts  0.71 us

profile of v6, /device:TPU:0, one launch (start us, length us, event | category | flops | bytes accessed | tf_op | source)
XLA Modules:
  0.0 22.5 jit_solution(8293659825249218393)
XLA Ops:
  0.7 21.2 %shard_map.64 = f32[32,2048]{1,0:T(8,128)S(1)} custom-call(f32[1,32,8192]{2,1,0:T(8,128)} %grad.1, f32[1,32,8192]{2,1,0:T(8,128)} %illum.1, s32[1]{0:T(128)S(6)} %copy.8.count, f32[1,2048]{1,0:T(1,128)} %bitcast.3, f32[1,64]{1,0:T(1,128)} %bitcast.4, s32[1,32]{1,0:T(1,128)} %bitcast.5), custom_call_target="tpu_custom_call" | custom-call | tf_op jit(solution)/shard_map/pallas_call | solution.py:432
  21.8 0.7 %copy.9 = f32[32,2048]{1,0:T(8,128)} copy(f32[32,2048]{1,0:T(8,128)S(1)} %shard_map.64) | data formatting | bytes 524288

commit v7 on v6

--- a/solution.py
+++ b/solution.py
@@ -364,12 +364,16 @@
                 tail = first(run)
             late[n][d, pl.ds(cols + j, 1), :] = tail[0:1]
         for j in range(ks - 1):
-            carry_copy(late[n], late_send, late_recv.at[n], j).start()
+            carry_copy(late[n], late_send, late_recv.at[int(n + 1 == len(turns))], j).start()
 
     others = pl.ds(0, ks - 1)
     wait_for(early.at[others], early_recv)
     for n, group in enumerate(turns):
-        wait_for(late[n].at[others], late_recv.at[n])
+        if n == 0:
+            most = width // LANES - reach_of(turns[-1])[1]
+            wait_for(early.at[others, :, pl.ds(0, most)], late_recv.at[0])
+        if n + 1 == len(turns):
+            wait_for(late[n].at[others], late_recv.at[1])
         start, cols = reach_of(group)
         rs = pl.ds(start, cols)
         down, lift = pl.ds(0, cols), pl.ds(cols, cols)
@@ -456,7 +460,7 @@
             dma,
             dma,
             dma,
-            dma((len(turns),)),
+            dma((2,)),
             dma,
             dma,
             dma((3,)),

time: 22.7 us -> 22.7 us (level)
  no operation moved by 1% of the time
where the time goes in v7:
time: 22.7 us; the launch traced here: 22.5 us
  Pallas kernels  21.1 us (93%)
  local copies, waits for them, and re-layouts  0.71 us (3%)
  between operations  0.66 us (3%)
    pallas_call x1, Pallas kernels, shards(): pl.pallas_call(functools.partial(body, (ys, ks, rows, width, chunks, load...  21.1 us
    unnamed x1, local copies, waits for them, and re-layouts  0.71 us

profile of v7, /device:TPU:0, one launch (start us, length us, event | category | flops | bytes accessed | tf_op | source)
XLA Modules:
  0.0 22.5 jit_solution(15607677698177005453)
XLA Ops:
  0.7 21.1 %shard_map.64 = f32[32,2048]{1,0:T(8,128)S(1)} custom-call(f32[1,32,8192]{2,1,0:T(8,128)} %grad.1, f32[1,32,8192]{2,1,0:T(8,128)} %illum.1, s32[1]{0:T(128)S(6)} %copy.8.count, f32[1,2048]{1,0:T(1,128)} %bitcast.3, f32[1,64]{1,0:T(1,128)} %bitcast.4, s32[1,32]{1,0:T(1,128)} %bitcast.5), custom_call_target="tpu_custom_call" | custom-call | tf_op jit(solution)/shard_map/pallas_call | solution.py:436
  21.8 0.7 %copy.9 = f32[32,2048]{1,0:T(8,128)} copy(f32[32,2048]{1,0:T(8,128)S(1)} %shard_map.64) | data formatting | bytes 524288

commit v8 on v5

--- a/solution.py
+++ b/solution.py
@@ -325,6 +325,8 @@
 
     for r in range(rounds):
         pass_on(r)
+    for r in relays:
+        forward(r)
     for j in range(ks - 1):
         carry_copy(early, early_send, early_recv, j).start()
 
@@ -355,15 +357,16 @@
                 tail = first(run)
             late[n][d, pl.ds(cols + j, 1), :] = tail[0:1]
         for j in range(ks - 1):
-            carry_copy(late[n], late_send, late_recv.at[n], j).start()
-        if n == 0:
-            for r in relays:
-                forward(r)
+            carry_copy(late[n], late_send, late_recv.at[int(n + 1 == len(turns))], j).start()
 
     others = pl.ds(0, ks - 1)
     wait_for(early.at[others], early_recv)
     for n, group in enumerate(turns):
-        wait_for(late[n].at[others], late_recv.at[n])
+        if n == 0:
+            most = width // LANES - reach_of(turns[-1])[1]
+            wait_for(early.at[others, :, pl.ds(0, most)], late_recv.at[0])
+        if n + 1 == len(turns):
+            wait_for(late[n].at[others], late_recv.at[1])
         start, cols = reach_of(group)
         rs = pl.ds(start, cols)
         down, lift = pl.ds(0, cols), pl.ds(cols, cols)
@@ -450,7 +453,7 @@
             dma,
             dma,
             dma,
-            dma((len(turns),)),
+            dma((2,)),
             dma,
             dma,
             dma((3,)),

time: 22.7 us -> 22.7 us (level)
  no operation moved by 1% of the time
where the time goes in v8:
time: 22.7 us; the launch traced here: 22.6 us
  Pallas kernels  21.2 us (93%)
  local copies, waits for them, and re-layouts  0.71 us (3%)
  between operations  0.66 us (3%)
    pallas_call x1, Pallas kernels, shards(): pl.pallas_call(functools.partial(body, (ys, ks, rows, width, chunks, load...  21.2 us
    unnamed x1, local copies, waits for them, and re-layouts  0.71 us

profile of v8, /device:TPU:0, one launch (start us, length us, event | category | flops | bytes accessed | tf_op | source)
XLA Modules:
  0.0 22.6 jit_solution(10863565760225970735)
XLA Ops:
  0.7 21.2 %shard_map.64 = f32[32,2048]{1,0:T(8,128)S(1)} custom-call(f32[1,32,8192]{2,1,0:T(8,128)} %grad.1, f32[1,32,8192]{2,1,0:T(8,128)} %illum.1, s32[1]{0:T(128)S(6)} %copy.8.count, f32[1,2048]{1,0:T(1,128)} %bitcast.3, f32[1,64]{1,0:T(1,128)} %bitcast.4, s32[1,32]{1,0:T(1,128)} %bitcast.5), custom_call_target="tpu_custom_call" | custom-call | tf_op jit(solution)/shard_map/pallas_call | solution.py:429
  21.9 0.7 %copy.9 = f32[32,2048]{1,0:T(8,128)} copy(f32[32,2048]{1,0:T(8,128)S(1)} %shard_map.64) | data formatting | bytes 524288
